TPU v7x, 512 devices: a whole 4x8x8 slice. The times are simulated.
512 devices in a mesh: dp: 64 (over y, z), fsdp: 8 (over x, core).
Axes of the slice: x: 4, y: 8, z: 8, core: 2. Of those that a mesh axis runs over, the one named last changes fastest.
Arguments:
- frames: bfloat16 [524288, 512], P(('dp', 'fsdp')), may hold values from -6 to 6
- utt_pairs: int32 [8, 64, 4], P('fsdp'), may hold values from 32 to 256, as said below
- utt_dest: int32 [8, 64, 4], P('fsdp'), may hold values from 0 to 63, as said below
- conv_weight: bfloat16 [1536, 512], P('dp'), may hold values from -0.15625 to 0.15625
- proj_weight: bfloat16 [512, 1536], P('dp'), may hold values from -0.25 to 0.25
- point_weight: bfloat16 [2, 1536, 1536], P(None, None, 'fsdp'), may hold values from -0.15625 to 0.15625
- depth_weight: float32 [31, 1536], replicated, may hold values from -1 to 1
- gain_first: float32 [1536], replicated, may hold values from 0.5 to 1.5
- gain_second: float32 [1536], replicated, may hold values from 0.5 to 1.5
Outputs:
- encoded: bfloat16 [262144, 1536], P(('dp', 'fsdp'))
Inputs may be any that keep to these rules, and one draw needn't show every extreme that they name: `utt_pairs`: every loader holds exactly 512 pairs and every sequence device receives exactly 512 pairs, from 4 different loaders. Each loader holds one utterance of exactly 256 pairs and one of exactly 32 pairs. `utt_dest`: the 4 utterances of loader i go to the 4 different sequence devices (i + k * 64 / 4) mod 64, k = 0 .. 3, in some order.
All inputs are finite; a program needn't handle non-finite values.
Results may differ from a plain program's by a relative error of at most 0.012.
Values may be sent and summed in bfloat16 or wider, within the bound.
No kernel may reach another device: no remote copies, remote signals or barrier semaphores. Data moves between devices by JAX's collectives and lax.ppermute only.
A program may use at most 64 MiB of HBM per device.

v0:
```python
import jax
import jax.numpy as jnp
from jax import lax
from jax.sharding import PartitionSpec as P


def passed_along(value, axis, steps):
    count = lax.axis_size(axis)
    pairs = [(source, (source + steps) % count) for source in range(count)]
    return lax.ppermute(value, axis, pairs)


def frontend(pair_rows, first_rows, conv_full):
    channels = pair_rows.shape[1] // 2
    even_frames = pair_rows[:, :channels]
    odd_frames = pair_rows[:, channels:]
    earlier = jnp.pad(odd_frames[:-1], ((1, 0), (0, 0)))
    earlier = jnp.where(first_rows[:, None], jnp.zeros_like(earlier), earlier)
    summed = jnp.dot(earlier, conv_full[:channels], preferred_element_type=jnp.float32)
    summed = summed + jnp.dot(
        even_frames, conv_full[channels : 2 * channels], preferred_element_type=jnp.float32
    )
    summed = summed + jnp.dot(
        odd_frames, conv_full[2 * channels :], preferred_element_type=jnp.float32
    )
    return jax.nn.relu(summed).astype(jnp.bfloat16)


def layer_norm(values, scales):
    centered = values - jnp.mean(values, axis=-1, keepdims=True)
    variance = jnp.mean(centered * centered, axis=-1, keepdims=True)
    return centered * lax.rsqrt(variance + 1e-05) * scales


def depthwise(gated, depth_weight, positions, lengths):
    row_count = gated.shape[0]
    kernel_size = depth_weight.shape[0]
    half_width = kernel_size // 2
    padded = jnp.pad(gated.astype(jnp.float32), ((half_width, half_width), (0, 0)))
    mixed = jnp.zeros(gated.shape, jnp.float32)
    for tap_index in range(kernel_size):
        offset = tap_index - half_width
        inside = (positions + offset >= 0) & (positions + offset < lengths)
        term = padded[tap_index : tap_index + row_count] * depth_weight[tap_index][None, :]
        mixed = mixed + jnp.where(inside[:, None], term, jnp.zeros_like(term))
    return mixed


def gate_product(normed, value_weight, gate_weight):
    value_part = jnp.dot(normed, value_weight, preferred_element_type=jnp.float32)
    gate_part = jnp.dot(normed, gate_weight, preferred_element_type=jnp.float32)
    return (value_part * jax.nn.sigmoid(gate_part)).astype(jnp.bfloat16)


def cut_pieces(source_rows, own_starts, slot_size, utt_count):
    padded = jnp.pad(source_rows, ((0, slot_size), (0, 0)))
    pieces = []
    for slot_index in range(utt_count):
        pieces.append(lax.dynamic_slice_in_dim(padded, own_starts[slot_index], slot_size, 0))
    return pieces


def body(
    frames,
    utt_pairs,
    utt_dest,
    conv_weight,
    proj_weight,
    point_weight,
    depth_weight,
    gain_first,
    gain_second,
):
    node_count = lax.axis_size("dp")
    own_index = lax.axis_index("dp")
    pair_count = frames.shape[0] // 2
    channels = frames.shape[1]
    utt_count = utt_pairs.shape[2]
    spacing = node_count // utt_count
    slot_size = pair_count // 2
    pair_table = utt_pairs[0]
    dest_table = utt_dest[0]
    loader_ids = jnp.arange(node_count, dtype=jnp.int32)
    slot_ids = jnp.arange(utt_count, dtype=jnp.int32)
    slot_table = (dest_table - loader_ids[:, None]) % node_count // spacing
    matches = (slot_table[:, :, None] == slot_ids[None, None, :]).astype(jnp.int32)
    loader_offsets = jnp.cumsum(pair_table, axis=1) - pair_table
    slot_counts = jnp.sum(matches * pair_table[:, :, None], axis=1)
    slot_starts = jnp.sum(matches * loader_offsets[:, :, None], axis=1)
    conv_full, proj_full = (
        lax.all_gather(conv_weight, "dp", axis=0, tiled=True),
        lax.all_gather(proj_weight, "dp", axis=0, tiled=True),
    )
    own_starts = slot_starts[own_index]
    sources = (own_index - slot_ids * spacing) % node_count
    piece_lengths = slot_counts[sources, slot_ids]
    earlier_pieces = (sources[None, :] < sources[:, None]).astype(jnp.int32)
    piece_offsets = jnp.sum(earlier_pieces * piece_lengths[None, :], axis=1)
    pair_rows = jnp.arange(pair_count, dtype=jnp.int32)
    inside = (
        (pair_rows[:, None] >= piece_offsets[None, :])
        & (pair_rows[:, None] < piece_offsets[None, :] + piece_lengths[None, :])
    ).astype(jnp.int32)
    piece_index = jnp.sum(inside * slot_ids[None, :], axis=1)
    positions = pair_rows - jnp.sum(inside * piece_offsets[None, :], axis=1)
    lengths = jnp.sum(inside * piece_lengths[None, :], axis=1)
    flat_slot = piece_index * slot_size + positions
    frame_pairs = frames.reshape(pair_count, 2 * channels)
    pieces = cut_pieces(frame_pairs, own_starts, slot_size, utt_count)
    arrived = [pieces[0]]
    for slot_index in range(1, utt_count):
        arrived.append(passed_along(pieces[slot_index], "dp", slot_index * spacing))
    stacked = jnp.concatenate(arrived, axis=0)
    packed = jnp.take(stacked, flat_slot, axis=0)
    front = frontend(packed, positions == 0, conv_full)
    projected = jnp.dot(front, proj_full, preferred_element_type=jnp.float32).astype(jnp.bfloat16)
    normed = layer_norm(projected.astype(jnp.float32), gain_first).astype(jnp.bfloat16)
    weight_part = lax.all_gather(point_weight, "fsdp", axis=2, tiled=True)
    gated = gate_product(normed, weight_part[0], weight_part[1])
    mixed = depthwise(gated, depth_weight, positions, lengths)
    scaled = layer_norm(mixed, gain_second)
    return (scaled * jax.nn.sigmoid(scaled)).astype(jnp.bfloat16)


def solution(mesh):
    in_specs = (
        P(("dp", "fsdp"), None),
        P("fsdp", None, None),
        P("fsdp", None, None),
        P("dp", None),
        P("dp", None),
        P(None, None, "fsdp"),
        P(),
        P(),
        P(),
    )
    out_specs = P(("dp", "fsdp"), None)
    return jax.shard_map(body, mesh=mesh, in_specs=in_specs, out_specs=out_specs, check_vma=False)
```

profile of v0, /device:TPU:1, one launch (start us, length us, event | category | flops | bytes accessed | tf_op | source)
XLA Modules:
  0.0 303.4 jit_solution(6321874885541037050)
XLA Ops:
  6.5 0.7 all-gather.4.cloned.1.call-update
  8.8 0.8 reduce_window_sum.11
  9.5 0.7 add_select_fusion
  16.7 1.4 reshape.518
  20.7 1.6 pad_dynamic-slice_fusion.3
  22.2 5.1 %collective-permute-start = (bf16[256,1024]{1,0:T(8,128)(2,1)S(1)}, bf16[256,1024]{1,0:T(8,128)(2,1)S(1)}, u32[]{:S(2)}, u32[]{:S(2)}) collective-permute-start(bf16[256,1024]{1,0:T(8,128)(2,1)S(1)} %get-tuple-element.44), channel_id=1, source_target_pairs={{0,128},{8,136},{16,144},{24,152},{32,160},{40,168},{48,176},{56,1... | collective-permute-start | bytes 1572872 | tf_op jit(solution)/shard_map/ppermute | solution.py:10
  27.3 5.7 %collective-permute-start.1 = (bf16[256,1024]{1,0:T(8,128)(2,1)S(1)}, bf16[256,1024]{1,0:T(8,128)(2,1)}, u32[]{:S(2)}, u32[]{:S(2)}) collective-permute-start(bf16[256,1024]{1,0:T(8,128)(2,1)S(1)} %get-tuple-element.45), channel_id=1, source_target_pairs={{0,256},{8,264},{16,272},{24,280},{32,288},{40,296},{48,304},{56,3... | collective-permute-start | bytes 1572872 | tf_op jit(solution)/shard_map/ppermute | solution.py:10
  33.0 5.0 %collective-permute-start.2 = (bf16[256,1024]{1,0:T(8,128)(2,1)S(1)}, bf16[256,1024]{1,0:T(8,128)(2,1)}, u32[]{:S(2)}, u32[]{:S(2)}) collective-permute-start(bf16[256,1024]{1,0:T(8,128)(2,1)S(1)} %get-tuple-element.46), channel_id=1, source_target_pairs={{0,384},{8,392},{16,400},{24,408},{32,416},{40,424},{48,432},{56,4... | collective-permute-start | bytes 1572872 | tf_op jit(solution)/shard_map/ppermute | solution.py:10
  39.0 0.8 slice_reduce_fusion.29
  40.2 1.1 collective-permute-done
  41.2 27.6 %collective-permute-done.1 = bf16[256,1024]{1,0:T(8,128)(2,1)} collective-permute-done((bf16[256,1024]{1,0:T(8,128)(2,1)S(1)}, bf16[256,1024]{1,0:T(8,128)(2,1)}, u32[]{:S(2)}, u32[]{:S(2)}) %collective-permute-start.1) | collective-permute-done | bytes 524320 | tf_op jit(solution)/shard_map/ppermute | solution.py:10
  68.8 11.9 %collective-permute-done.2 = bf16[256,1024]{1,0:T(8,128)(2,1)} collective-permute-done((bf16[256,1024]{1,0:T(8,128)(2,1)S(1)}, bf16[256,1024]{1,0:T(8,128)(2,1)}, u32[]{:S(2)}, u32[]{:S(2)}) %collective-permute-start.2) | collective-permute-done | bytes 524320 | tf_op jit(solution)/shard_map/ppermute | solution.py:10
  80.7 1.5 pad_maximum_fusion
  82.3 2.2 gather_fusion.1
  84.7 31.2 %all-gather.4.cloned.1.call-done = bf16[1536,512]{1,0:T(8,128)(2,1)} async-done(((bf16[24,512]{1,0:T(8,128)(2,1)}), bf16[1536,512]{1,0:T(8,128)(2,1)}) %all-gather.4.cloned.1.call-update) | async-done | bytes 1572880 | tf_op jit(solution)/shard_map/all_gather | solution.py:91
  116.0 1.5 fusion.62
  117.5 2.5 convolution_add_fusion.1
  120.0 78.9 %all-gather.6.cloned.1.call-done = bf16[512,1536]{1,0:T(8,128)(2,1)} async-done(((bf16[8,1536]{1,0:T(8,128)(2,1)}), bf16[512,1536]{1,0:T(8,128)(2,1)}) %all-gather.6.cloned.1.call-update) | async-done | bytes 1572880 | tf_op jit(solution)/shard_map/all_gather | solution.py:92
  198.9 3.2 %convert_reduce_fusion = (f32[512]{0:T(512)S(1)}, bf16[512,1536]{1,0:T(8,128)(2,1)S(1)}) fusion(bf16[512,1536]{1,0:T(8,128)(2,1)} %all-gather.6.cloned.1.call-done, f32[512,512]{1,0:T(8,128)} %convolution_add_fusion.1, bf16[1536,512]{1,0:T(8,128)(2,1)} %all-gather.4.cloned.1.call-done, bf16[512,1024]{1,0:T(8,128)(2,1)S(1)} %broadcast_select_fusion), kind=kOutput, calls=%fused_computation.7 | convolution fusion | flops 1076887040 | bytes 5244928 | tf_op jit(solution)/shard_map/dot_general | solution.py:116
  202.7 59.3 %all-gather.8.cloned.1.call-done = bf16[2,1536,1536]{1,2,0:T(8,128)(2,1)} async-done(((bf16[2,1536,192]{1,2,0:T(8,128)(2,1)}), bf16[2,1536,1536]{1,2,0:T(8,128)(2,1)}) %all-gather.8.cloned.1.call-update) | async-done | bytes 9437200 | tf_op jit(solution)/shard_map/all_gather | solution.py:118
  261.9 5.2 %fusion.7 = f32[512,1536]{1,0:T(8,128)S(1)} fusion(bf16[2,1536,1536]{1,2,0:T(8,128)(2,1)} %all-gather.8.cloned.1.call-done, bf16[512,1536]{1,0:T(8,128)(2,1)S(1)} %get-tuple-element.85, f32[1536]{0:T(1024)S(1)} %copy-done.10, f32[512]{0:T(512)S(1)} %add_rsqrt_fusion.1, f32[512]{0:T(512)S(1)} %broadcast_multiply_fusion.1), kind=kOutput, calls=%fused_computation.13 | convolution fusion | flops 2421424128 | bytes 9447424 | tf_op jit(solution)/shard_map/dot_general | solution.py:51
  267.2 2.7 fusion.53
  269.9 24.0 %fusion.83 = (f32[512]{0:T(512)S(1)}, f32[512,1536]{1,0:T(8,128)S(1)}) fusion(f32[1536]{0:T(1024)S(1)} %copy-done.6, pred[512]{0:T(512)(128)(4,1)S(1)} %get-tuple-element.48, f32[1536]{0:T(1024)S(1)} %copy-done.7, pred[512]{0:T(512)(128)(4,1)S(1)} %get-tuple-element.49, f32[1536]{0:T(1024)S(1)} %get-tuple-element.6, ...), kind=kLoop, calls=%fused_computation.211 | loop fusion | flops 73137664 | bytes 6499840 | tf_op jit(solution)/shard_map/reduce_sum | solution.py:30
  294.6 2.2 multiply_convert_fusion
  (49 shorter events, 5.7 us)
Async XLA Ops:
  6.5 109.4 %all-gather.4.cloned.1.call-start = ((), (), s32[]{:S(2)}) async-start(), calls=%async_computation | async-start | bytes 1597440 | tf_op jit(solution)/shard_map/all_gather | solution.py:91
  7.3 191.6 %all-gather.6.cloned.1.call-start = ((), (), s32[]{:S(2)}) async-start(), calls=%async_computation.1 | async-start | bytes 1597440 | tf_op jit(solution)/shard_map/all_gather | solution.py:92
  8.0 253.9 %all-gather.8.cloned.1.call-start = ((), (), s32[]{:S(2)}) async-start(), calls=%async_computation.2 | async-start | bytes 10616832 | tf_op jit(solution)/shard_map/all_gather | solution.py:118
  8.7 30.2 %copy-start.1 = (f32[31,1536]{1,0:T(8,128)S(1)}, f32[31,1536]{1,0:T(8,128)}, u32[]{:S(2)}) copy-start(f32[31,1536]{1,0:T(8,128)} %param.15) | copy-start | bytes 571396
  22.2 19.0 %collective-permute-start = (bf16[256,1024]{1,0:T(8,128)(2,1)S(1)}, bf16[256,1024]{1,0:T(8,128)(2,1)S(1)}, u32[]{:S(2)}, u32[]{:S(2)}) collective-permute-start(bf16[256,1024]{1,0:T(8,128)(2,1)S(1)} %get-tuple-element.44), channel_id=1, source_target_pairs={{0,128},{8,136},{16,144},{24,152},{32,160},{40,168},{48,176},{56,1... | collective-permute-start | bytes 1572872 | tf_op jit(solution)/shard_map/ppermute | solution.py:10
  27.3 41.5 %collective-permute-start.1 = (bf16[256,1024]{1,0:T(8,128)(2,1)S(1)}, bf16[256,1024]{1,0:T(8,128)(2,1)}, u32[]{:S(2)}, u32[]{:S(2)}) collective-permute-start(bf16[256,1024]{1,0:T(8,128)(2,1)S(1)} %get-tuple-element.45), channel_id=1, source_target_pairs={{0,256},{8,264},{16,272},{24,280},{32,288},{40,296},{48,304},{56,3... | collective-permute-start | bytes 1572872 | tf_op jit(solution)/shard_map/ppermute | solution.py:10
  33.0 47.8 %collective-permute-start.2 = (bf16[256,1024]{1,0:T(8,128)(2,1)S(1)}, bf16[256,1024]{1,0:T(8,128)(2,1)}, u32[]{:S(2)}, u32[]{:S(2)}) collective-permute-start(bf16[256,1024]{1,0:T(8,128)(2,1)S(1)} %get-tuple-element.46), channel_id=1, source_target_pairs={{0,384},{8,392},{16,400},{24,408},{32,416},{40,424},{48,432},{56,4... | collective-permute-start | bytes 1572872 | tf_op jit(solution)/shard_map/ppermute | solution.py:10
  41.2 39.5 %copy-start = (bf16[256,1024]{1,0:T(8,128)(2,1)}, bf16[256,1024]{1,0:T(8,128)(2,1)S(1)}, u32[]{:S(2)}) copy-start(bf16[256,1024]{1,0:T(8,128)(2,1)S(1)} %collective-permute-done) | copy-start | bytes 1572868
  120.0 142.0 %copy-start.10 = (f32[1536]{0:T(1024)S(1)}, f32[1536]{0:T(1024)}, u32[]{:S(2)}) copy-start(f32[1536]{0:T(1024)} %param.16) | copy-start | bytes 18436
  261.9 5.2 %copy-start.9 = (bf16[2,1536,1536]{1,2,0:T(8,128)(2,1)S(1)}, bf16[2,1536,1536]{1,2,0:T(8,128)(2,1)}, u32[]{:S(2)}) copy-start(bf16[2,1536,1536]{1,2,0:T(8,128)(2,1)} %all-gather.8.cloned.1.call-done) | copy-start | bytes 28311556
  267.1 2.8 copy-start.2
  267.1 2.8 copy-start.3
  267.1 2.8 copy-start.4
  267.2 2.8 copy-start.5
  267.2 2.8 copy-start.6
  267.2 2.8 copy-start.7
  293.9 0.7 copy-start.8
Sparse Core Ops, SparseCore 0:
  10.4 105.5 all-gather.3
  119.0 79.7 all-gather.5
  201.0 60.9 all-gather.7
where the time goes:
time: 304 us; the launch traced here: 303 us
  waiting for transfers between devices  212 us (70%)
  other arithmetic  31.5 us (10%)
  between operations  21 us (7%)
  starting transfers between devices  15.8 us (5%)
  matrix products  15 us (5%)
  local copies, waits for them, and re-layouts  7.95 us (3%)
    all_gather x1, waiting for transfers between devices, body(): lax.all_gather(proj_weight, 'dp', axis=0, tiled=True)  78.9 us
    all_gather x1, waiting for transfers between devices, body(): weight_part = lax.all_gather(point_weight, 'fsdp', axis=2, tiled=True)  59.3 us
    ppermute x3, waiting for transfers between devices, passed_along(): return lax.ppermute(value, axis, pairs)  40.6 us
    all_gather x1, waiting for transfers between devices, body(): lax.all_gather(conv_weight, 'dp', axis=0, tiled=True)  31.2 us
    reduce_sum x1, other arithmetic, layer_norm(): centered = values - jnp.mean(values, axis=-1, keepdims=True)  24 us
    ppermute x3, starting transfers between devices, passed_along(): return lax.ppermute(value, axis, pairs)  15.7 us
  transfers between devices with their start and end apart: 6, of which 6 were waited for; matrix products, arithmetic and copies ran while one was open for 7% of the time, Pallas kernels for 0%

commit v1 on v0

--- a/solution.py
+++ b/solution.py
@@ -2,6 +2,12 @@
 import jax.numpy as jnp
 from jax import lax
 from jax.sharding import PartitionSpec as P
+
+
+def joined_along(tiles, dim):
+    tiles = jnp.moveaxis(tiles, 0, dim)
+    lengths = tiles.shape
+    return tiles.reshape(*lengths[:dim], lengths[dim] * lengths[dim + 1], *lengths[dim + 2 :])
 
 
 def passed_along(value, axis, steps):
@@ -115,7 +121,19 @@
     front = frontend(packed, positions == 0, conv_full)
     projected = jnp.dot(front, proj_full, preferred_element_type=jnp.float32).astype(jnp.bfloat16)
     normed = layer_norm(projected.astype(jnp.float32), gain_first).astype(jnp.bfloat16)
-    weight_part = lax.all_gather(point_weight, "fsdp", axis=2, tiled=True)
+    count_2 = lax.axis_size("fsdp")
+    pairs_2 = [(i, (i + 1) % count_2) for i in range(count_2)]
+    back = [(b, a) for a, b in pairs_2]
+    lower, upper = ([], [])
+    for turn in range(count_2 - 1):
+        if turn % 2 == 0:
+            lower.append(lax.ppermute(lower[-1] if lower else point_weight, "fsdp", pairs_2))
+        else:
+            upper.append(lax.ppermute(upper[-1] if upper else point_weight, "fsdp", back))
+    parts = jnp.stack([*lower[::-1], point_weight, *upper])
+    shift = lax.axis_index("fsdp") - len(lower)
+    parts = parts[(jnp.arange(count_2) - shift) % count_2]
+    weight_part = joined_along(parts, 2)
     gated = gate_product(normed, weight_part[0], weight_part[1])
     mixed = depthwise(gated, depth_weight, positions, lengths)
     scaled = layer_norm(mixed, gain_second)

time: 304 us -> 279 us (0.918); the launches traced: 303 us -> 275 us
  waiting for transfers between devices: 212 us -> 138 us
  local copies, waits for them, and re-layouts: 7.95 us -> 39.1 us
  starting transfers between devices: 15.8 us -> 28 us
    all_gather x1 -> x0, waiting for transfers between devices: 59.3 us -> none  [body(): weight_part = lax.all_gather(point_weight, 'fsdp', axis=2, tiled=True)]
    ppermute x3, waiting for transfers between devices: 40.6 us -> 16 us  [passed_along(): return lax.ppermute(value, axis, pairs)]
    ppermute x0 -> x7, starting transfers between devices: none -> 18.5 us  [the longest x4 13.5 us: body(): lax.ppermute(lower[-1] if lower else point_weight, 'fsdp', pairs_2)]
    unnamed x22 -> x37, local copies, waits for them, and re-layouts: 0.26 us -> 15.7 us
    ppermute x0 -> x7, waiting for transfers between devices: none -> 10.4 us  [the longest x4 10.3 us: body(): lax.ppermute(lower[-1] if lower else point_weight, 'fsdp', pairs_2)]
    gather x0 -> x1, local copies, waits for them, and re-layouts: none -> 9.02 us  [body(): parts = parts[(jnp.arange(count_2) - shift) % count_2]]
    all_gather x1, waiting for transfers between devices: 31.2 us -> 38.1 us  [body(): lax.all_gather(conv_weight, 'dp', axis=0, tiled=True)]
    ppermute x3, starting transfers between devices: 15.7 us -> 9.52 us  [passed_along(): return lax.ppermute(value, axis, pairs)]
  transfers between devices with their start and end apart: 6 -> 12, of which waited for: 6 -> 5; matrix products, arithmetic and copies ran while one was open for 7% -> 14% of each run, Pallas kernels for 0% -> 0%
where the time goes in v1:
time: 279 us; the launch traced here: 275 us
  waiting for transfers between devices  138 us (49%)
  local copies, waits for them, and re-layouts  39.1 us (14%)
  other arithmetic  34.2 us (12%)
  starting transfers between devices  28 us (10%)
  between operations  21.2 us (8%)
  matrix products  14.5 us (5%)
    all_gather x1, waiting for transfers between devices, body(): lax.all_gather(proj_weight, 'dp', axis=0, tiled=True)  73.1 us
    all_gather x1, waiting for transfers between devices, body(): lax.all_gather(conv_weight, 'dp', axis=0, tiled=True)  38.1 us
    reduce_sum x1, other arithmetic, layer_norm(): centered = values - jnp.mean(values, axis=-1, keepdims=True)  24.2 us
    ppermute x3, waiting for transfers between devices, passed_along(): return lax.ppermute(value, axis, pairs)  16 us
    unnamed x37, local copies, waits for them, and re-layouts  15.7 us
    ppermute x4, starting transfers between devices, body(): lax.ppermute(lower[-1] if lower else point_weight, 'fsdp', pairs_2)  13.5 us
    ppermute x4, waiting for transfers between devices, body(): lax.ppermute(lower[-1] if lower else point_weight, 'fsdp', pairs_2)  10.3 us
    ppermute x3, starting transfers between devices, passed_along(): return lax.ppermute(value, axis, pairs)  9.52 us
  transfers between devices with their start and end apart: 12, of which 5 were waited for; matrix products, arithmetic and copies ran while one was open for 14% of the time, Pallas kernels for 0%

profile of v1, /device:TPU:1, one launch (start us, length us, event | category | flops | bytes accessed | tf_op | source)
XLA Modules:
  0.0 275.3 jit_solution(2112608723777516423)
XLA Ops:
  7.3 2.6 collective-permute-start.3
  9.9 4.3 %collective-permute-start.7 = (bf16[2,1536,192]{1,2,0:T(8,128)(2,1)}, bf16[2,1536,192]{1,2,0:T(8,128)(2,1)}, u32[]{:S(2)}, u32[]{:S(2)}) collective-permute-start(bf16[2,1536,192]{1,2,0:T(8,128)(2,1)} %param.14), channel_id=1, source_target_pairs={{1,0},{2,1},{3,2},{4,3},{5,4},{6,5},{7,6},{0,7},{9,8},{10,9},{11,1... | collective-permute-start | bytes 3538952 | tf_op jit(solution)/shard_map/ppermute | solution.py:132
  29.5 3.2 %collective-permute-start.1 = (bf16[256,1024]{1,0:T(8,128)(2,1)S(1)}, bf16[256,1024]{1,0:T(8,128)(2,1)S(1)}, u32[]{:S(2)}, u32[]{:S(2)}) collective-permute-start(bf16[256,1024]{1,0:T(8,128)(2,1)S(1)} %get-tuple-element.47), channel_id=1, source_target_pairs={{0,256},{8,264},{16,272},{24,280},{32,288},{40,296},{48,304},{56,3... | collective-permute-start | bytes 1572872 | tf_op jit(solution)/shard_map/ppermute | solution.py:16
  32.7 4.4 %collective-permute-start = (bf16[256,1024]{1,0:T(8,128)(2,1)S(1)}, bf16[256,1024]{1,0:T(8,128)(2,1)}, u32[]{:S(2)}, u32[]{:S(2)}) collective-permute-start(bf16[256,1024]{1,0:T(8,128)(2,1)S(1)} %get-tuple-element.46), channel_id=1, source_target_pairs={{0,128},{8,136},{16,144},{24,152},{32,160},{40,168},{48,176},{56,1... | collective-permute-start | bytes 1572872 | tf_op jit(solution)/shard_map/ppermute | solution.py:16
  37.1 2.6 collective-permute-start.4
  42.8 10.3 %collective-permute-done.4 = bf16[2,1536,192]{1,2,0:T(8,128)(2,1)} collective-permute-done((bf16[2,1536,192]{1,2,0:T(8,128)(2,1)}, bf16[2,1536,192]{1,2,0:T(8,128)(2,1)}, u32[]{:S(2)}, u32[]{:S(2)}) %collective-permute-start.4) | collective-permute-done | bytes 1179680 | tf_op jit(solution)/shard_map/ppermute | solution.py:130
  53.2 2.5 collective-permute-start.5
  57.4 13.8 %collective-permute-done.2 = bf16[256,1024]{1,0:T(8,128)(2,1)S(1)} collective-permute-done((bf16[256,1024]{1,0:T(8,128)(2,1)S(1)}, bf16[256,1024]{1,0:T(8,128)(2,1)S(1)}, u32[]{:S(2)}, u32[]{:S(2)}) %collective-permute-start.2) | collective-permute-done | bytes 524320 | tf_op jit(solution)/shard_map/ppermute | solution.py:16
  77.7 38.1 %all-gather.3.cloned.1.call-done = bf16[1536,512]{1,0:T(8,128)(2,1)} async-done(((bf16[24,512]{1,0:T(8,128)(2,1)}), bf16[1536,512]{1,0:T(8,128)(2,1)}) %all-gather.3.cloned.1.call-update) | async-done | bytes 1572880 | tf_op jit(solution)/shard_map/all_gather | solution.py:97
  117.4 5.8 %collective-permute-start.6 = (bf16[2,1536,192]{1,2,0:T(8,128)(2,1)}, bf16[2,1536,192]{1,2,0:T(8,128)(2,1)}, u32[]{:S(2)}, u32[]{:S(2)}) collective-permute-start(bf16[2,1536,192]{1,2,0:T(8,128)(2,1)} %collective-permute-done.5), channel_id=1, source_target_pairs={{0,1},{1,2},{2,3},{3,4},{4,5},{5,6},{6,7},{7,0},{8,9},{9,10},{10,1... | collective-permute-start | bytes 3538952 | tf_op jit(solution)/shard_map/ppermute | solution.py:130
  123.2 2.4 convolution_add_fusion.1
  125.6 73.1 %all-gather.5.cloned.1.call-done = bf16[512,1536]{1,0:T(8,128)(2,1)} async-done(((bf16[8,1536]{1,0:T(8,128)(2,1)}), bf16[512,1536]{1,0:T(8,128)(2,1)}) %all-gather.5.cloned.1.call-update) | async-done | bytes 1572880 | tf_op jit(solution)/shard_map/all_gather | solution.py:98
  198.7 3.2 %convert_reduce_fusion = (f32[512]{0:T(512)S(1)}, bf16[512,1536]{1,0:T(8,128)(2,1)S(1)}) fusion(bf16[512,1536]{1,0:T(8,128)(2,1)} %all-gather.5.cloned.1.call-done, f32[512,512]{1,0:T(8,128)} %convolution_add_fusion.1, bf16[1536,512]{1,0:T(8,128)(2,1)} %all-gather.3.cloned.1.call-done, bf16[512,1024]{1,0:T(8,128)(2,1)S(1)} %broadcast_select_fusion), kind=kOutput, calls=%fused_computation.4 | convolution fusion | flops 1076887040 | bytes 5244928 | tf_op jit(solution)/shard_map/dot_general | solution.py:122
  202.6 2.4 bitcast_dynamic-update-slice_fusion.7
  204.9 2.5 bitcast_dynamic-update-slice_fusion.6
  207.4 2.4 bitcast_dynamic-update-slice_fusion.5
  213.2 2.4 bitcast_dynamic-update-slice_fusion.2
  215.6 2.4 bitcast_dynamic-update-slice_fusion.1
  218.0 2.5 bitcast_dynamic-update-slice_fusion
  220.4 9.0 %gather_fusion.2 = bf16[8,2,1536,192]{2,3,1,0:T(8,128)(2,1)} fusion(bf16[8,2,1536,192]{2,3,1,0:T(8,128)(2,1)} %bitcast_dynamic-update-slice_fusion, s32[1024]{0:T(1024)} %pad_clamp_fusion), kind=kCustom, calls=%fused_computation.2 | custom fusion | bytes 18874400 | tf_op jit(solution)/shard_map/gather | solution.py:135
  229.5 4.4 %fusion.83 = (bf16[1,1536,8,192]{1,3,0,2:T(8,128)(2,1)S(1)}, bf16[1,1536,8,192]{1,3,0,2:T(8,128)(2,1)S(1)}) fusion(bf16[2,1536,8,192]{1,3,0,2:T(8,128)(2,1)} %bitcast.43), kind=kLoop, calls=%fused_computation.225 | loop fusion | bytes 18874368 | tf_op jit(solution)/shard_map/slice | solution.py:137
  233.9 4.6 %fusion.4 = f32[512,1536]{1,0:T(8,128)S(1)} fusion(bf16[1536,1536]{0,1:T(8,128)(2,1)S(1)} %bitcast.45, bf16[512,1536]{1,0:T(8,128)(2,1)} %copy-done, f32[1536]{0:T(1024)S(1)} %copy-done.14, f32[512]{0:T(512)S(1)} %add_rsqrt_fusion.1, f32[512]{0:T(512)S(1)} %broadcast_multiply_fusion.1), kind=kOutput, calls=%fused_computation.11 | convolution fusion | flops 2422210560 | bytes 9447424 | tf_op jit(solution)/shard_map/dot_general | solution.py:57
  238.5 2.8 fusion.50
  241.3 24.2 %fusion.82 = (f32[512]{0:T(512)S(1)}, f32[512,1536]{1,0:T(8,128)S(1)}) fusion(f32[1536]{0:T(1024)S(1)} %copy-done.10, pred[512]{0:T(512)(128)(4,1)S(1)} %get-tuple-element.50, f32[1536]{0:T(1024)S(1)} %copy-done.11, pred[512]{0:T(512)(128)(4,1)S(1)} %get-tuple-element.51, f32[1536]{0:T(1024)S(1)} %get-tuple-element.6, ...), kind=kLoop, calls=%fused_computation.224 | loop fusion | flops 73137664 | bytes 6499840 | tf_op jit(solution)/shard_map/reduce_sum | solution.py:36
  (80 shorter events, 28.4 us)
Async XLA Ops:
  6.5 34.9 %copy-start.5 = (f32[31,1536]{1,0:T(8,128)S(1)}, f32[31,1536]{1,0:T(8,128)}, u32[]{:S(2)}) copy-start(f32[31,1536]{1,0:T(8,128)} %param.15) | copy-start | bytes 571396
  6.5 109.3 %all-gather.3.cloned.1.call-start = ((), (), s32[]{:S(2)}) async-start(), calls=%async_computation | async-start | bytes 1597440 | tf_op jit(solution)/shard_map/all_gather | solution.py:97
  7.3 191.5 %all-gather.5.cloned.1.call-start = ((), (), s32[]{:S(2)}) async-start(), calls=%async_computation.1 | async-start | bytes 1597440 | tf_op jit(solution)/shard_map/all_gather | solution.py:98
  7.3 29.8 %collective-permute-start.3 = (bf16[2,1536,192]{1,2,0:T(8,128)(2,1)}, bf16[2,1536,192]{1,2,0:T(8,128)(2,1)}, u32[]{:S(2)}, u32[]{:S(2)}) collective-permute-start(bf16[2,1536,192]{1,2,0:T(8,128)(2,1)} %param.14), channel_id=1, source_target_pairs={{0,1},{1,2},{2,3},{3,4},{4,5},{5,6},{6,7},{7,0},{8,9},{9,10},{10,1... | collective-permute-start | bytes 3538952 | tf_op jit(solution)/shard_map/ppermute | solution.py:130
  9.9 31.4 %collective-permute-start.7 = (bf16[2,1536,192]{1,2,0:T(8,128)(2,1)}, bf16[2,1536,192]{1,2,0:T(8,128)(2,1)}, u32[]{:S(2)}, u32[]{:S(2)}) collective-permute-start(bf16[2,1536,192]{1,2,0:T(8,128)(2,1)} %param.14), channel_id=1, source_target_pairs={{1,0},{2,1},{3,2},{4,3},{5,4},{6,5},{7,6},{0,7},{9,8},{10,9},{11,1... | collective-permute-start | bytes 3538952 | tf_op jit(solution)/shard_map/ppermute | solution.py:132
  27.6 43.6 %collective-permute-start.2 = (bf16[256,1024]{1,0:T(8,128)(2,1)S(1)}, bf16[256,1024]{1,0:T(8,128)(2,1)S(1)}, u32[]{:S(2)}, u32[]{:S(2)}) collective-permute-start(bf16[256,1024]{1,0:T(8,128)(2,1)S(1)} %get-tuple-element.48), channel_id=1, source_target_pairs={{0,384},{8,392},{16,400},{24,408},{32,416},{40,424},{48,432},{56,4... | collective-permute-start | bytes 1572872 | tf_op jit(solution)/shard_map/ppermute | solution.py:16
  29.5 41.6 %collective-permute-start.1 = (bf16[256,1024]{1,0:T(8,128)(2,1)S(1)}, bf16[256,1024]{1,0:T(8,128)(2,1)S(1)}, u32[]{:S(2)}, u32[]{:S(2)}) collective-permute-start(bf16[256,1024]{1,0:T(8,128)(2,1)S(1)} %get-tuple-element.47), channel_id=1, source_target_pairs={{0,256},{8,264},{16,272},{24,280},{32,288},{40,296},{48,304},{56,3... | collective-permute-start | bytes 1572872 | tf_op jit(solution)/shard_map/ppermute | solution.py:16
  32.7 40.6 %collective-permute-start = (bf16[256,1024]{1,0:T(8,128)(2,1)S(1)}, bf16[256,1024]{1,0:T(8,128)(2,1)}, u32[]{:S(2)}, u32[]{:S(2)}) collective-permute-start(bf16[256,1024]{1,0:T(8,128)(2,1)S(1)} %get-tuple-element.46), channel_id=1, source_target_pairs={{0,128},{8,136},{16,144},{24,152},{32,160},{40,168},{48,176},{56,1... | collective-permute-start | bytes 1572872 | tf_op jit(solution)/shard_map/ppermute | solution.py:16
  37.1 16.1 %collective-permute-start.4 = (bf16[2,1536,192]{1,2,0:T(8,128)(2,1)}, bf16[2,1536,192]{1,2,0:T(8,128)(2,1)}, u32[]{:S(2)}, u32[]{:S(2)}) collective-permute-start(bf16[2,1536,192]{1,2,0:T(8,128)(2,1)} %collective-permute-done.3), channel_id=1, source_target_pairs={{0,1},{1,2},{2,3},{3,4},{4,5},{5,6},{6,7},{7,0},{8,9},{9,10},{10,1... | collective-permute-start | bytes 3538952 | tf_op jit(solution)/shard_map/ppermute | solution.py:130
  41.3 35.9 %collective-permute-start.8 = (bf16[2,1536,192]{1,2,0:T(8,128)(2,1)}, bf16[2,1536,192]{1,2,0:T(8,128)(2,1)}, u32[]{:S(2)}, u32[]{:S(2)}) collective-permute-start(bf16[2,1536,192]{1,2,0:T(8,128)(2,1)} %collective-permute-done.7), channel_id=1, source_target_pairs={{1,0},{2,1},{3,2},{4,3},{5,4},{6,5},{7,6},{0,7},{9,8},{10,9},{11,1... | collective-permute-start | bytes 3538952 | tf_op jit(solution)/shard_map/ppermute | solution.py:132
  53.2 64.2 %collective-permute-start.5 = (bf16[2,1536,192]{1,2,0:T(8,128)(2,1)}, bf16[2,1536,192]{1,2,0:T(8,128)(2,1)}, u32[]{:S(2)}, u32[]{:S(2)}) collective-permute-start(bf16[2,1536,192]{1,2,0:T(8,128)(2,1)} %collective-permute-done.4), channel_id=1, source_target_pairs={{0,1},{1,2},{2,3},{3,4},{4,5},{5,6},{6,7},{7,0},{8,9},{9,10},{10,1... | collective-permute-start | bytes 3538952 | tf_op jit(solution)/shard_map/ppermute | solution.py:130
  56.6 18.3 %copy-start.12 = (s32[1024]{0:T(1024)S(1)}, s32[1024]{0:T(1024)}, u32[]{:S(2)}) copy-start(s32[1024]{0:T(1024)} %pad_clamp_fusion.1) | copy-start | bytes 12292
  77.2 140.8 %collective-permute-start.9 = (bf16[2,1536,192]{1,2,0:T(8,128)(2,1)}, bf16[2,1536,192]{1,2,0:T(8,128)(2,1)}, u32[]{:S(2)}, u32[]{:S(2)}) collective-permute-start(bf16[2,1536,192]{1,2,0:T(8,128)(2,1)} %collective-permute-done.8), channel_id=1, source_target_pairs={{1,0},{2,1},{3,2},{4,3},{5,4},{6,5},{7,6},{0,7},{9,8},{10,9},{11,1... | collective-permute-start | bytes 3538952 | tf_op jit(solution)/shard_map/ppermute | solution.py:132
  117.4 85.2 %collective-permute-start.6 = (bf16[2,1536,192]{1,2,0:T(8,128)(2,1)}, bf16[2,1536,192]{1,2,0:T(8,128)(2,1)}, u32[]{:S(2)}, u32[]{:S(2)}) collective-permute-start(bf16[2,1536,192]{1,2,0:T(8,128)(2,1)} %collective-permute-done.5), channel_id=1, source_target_pairs={{0,1},{1,2},{2,3},{3,4},{4,5},{5,6},{6,7},{7,0},{8,9},{9,10},{10,1... | collective-permute-start | bytes 3538952 | tf_op jit(solution)/shard_map/ppermute | solution.py:130
  202.0 18.5 %copy-start = (bf16[512,1536]{1,0:T(8,128)(2,1)}, bf16[512,1536]{1,0:T(8,128)(2,1)S(1)}, u32[]{:S(2)}) copy-start(bf16[512,1536]{1,0:T(8,128)(2,1)S(1)} %get-tuple-element.87) | copy-start | bytes 4718596
  204.9 7.2 %copy-start.2 = (bf16[2,1536,192]{1,2,0:T(8,128)(2,1)S(1)}, bf16[2,1536,192]{1,2,0:T(8,128)(2,1)}, u32[]{:S(2)}) copy-start(bf16[2,1536,192]{1,2,0:T(8,128)(2,1)} %param.14) | copy-start | bytes 3538948
  229.5 4.4 %copy-start.14 = (f32[1536]{0:T(1024)S(1)}, f32[1536]{0:T(1024)}, u32[]{:S(2)}) copy-start(f32[1536]{0:T(1024)} %param.16) | copy-start | bytes 18436
  233.9 4.6 %copy-start.1 = (bf16[512,1536]{1,0:T(8,128)(2,1)S(1)}, bf16[512,1536]{1,0:T(8,128)(2,1)}, u32[]{:S(2)}) copy-start(bf16[512,1536]{1,0:T(8,128)(2,1)} %copy-done) | copy-start | bytes 4718596
  238.5 2.8 %copy-start.6 = (f32[1536]{0:T(1024)S(1)}, f32[1536]{0:T(1024)}, u32[]{:S(2)}) copy-start(f32[1536]{0:T(1024)} %get-tuple-element.30) | copy-start | bytes 18436
  238.5 2.8 %copy-start.7 = (f32[1536]{0:T(1024)S(1)}, f32[1536]{0:T(1024)}, u32[]{:S(2)}) copy-start(f32[1536]{0:T(1024)} %get-tuple-element.31) | copy-start | bytes 18436
  238.5 2.8 %copy-start.8 = (f32[1536]{0:T(1024)S(1)}, f32[1536]{0:T(1024)}, u32[]{:S(2)}) copy-start(f32[1536]{0:T(1024)} %get-tuple-element.32) | copy-start | bytes 18436
  238.5 2.8 %copy-start.9 = (f32[1536]{0:T(1024)S(1)}, f32[1536]{0:T(1024)}, u32[]{:S(2)}) copy-start(f32[1536]{0:T(1024)} %get-tuple-element.33) | copy-start | bytes 18436
  238.5 2.8 %copy-start.10 = (f32[1536]{0:T(1024)S(1)}, f32[1536]{0:T(1024)}, u32[]{:S(2)}) copy-start(f32[1536]{0:T(1024)} %get-tuple-element.34) | copy-start | bytes 18436
  238.5 2.8 %copy-start.11 = (f32[1536]{0:T(1024)S(1)}, f32[1536]{0:T(1024)}, u32[]{:S(2)}) copy-start(f32[1536]{0:T(1024)} %get-tuple-element.35) | copy-start | bytes 18436
  (3 other events, 5.1 us)
Sparse Core Ops, SparseCore 0:
  10.4 105.3 all-gather.2
  118.9 79.7 all-gather.4
